TPU v7x, 512 devices: a whole 4x4x16 slice. The times are simulated.
512 devices in a mesh: row: 16 (over z_lo, core), col: 16 (over y, x), gz: 2 (over z_hi).
Axes of the slice: x: 4, y: 4, z: 16 (z_hi: 2, z_lo: 8; z = z_hi * 8 + z_lo), core: 2. Of those that a mesh axis runs over, the one named last changes fastest.
Arguments:
- modes: bfloat16 [64, 96, 32, 3, 2048], P('row', 'col', 'gz'), may hold values from -0.109375 to 0.109375
- blocks: float32 [8, 7, 3, 3], replicated, may hold values from -6 to 6
- material: int32 [64, 96, 32], P('row', 'col', 'gz'), may hold values from 0 to 7
Outputs:
- reduced: float32 [2048, 256], P('col')
All inputs are finite; a program needn't handle non-finite values.
Results may differ from a plain program's by a relative error of at most 0.0029.
Values may be sent and summed in bfloat16 or wider, within the bound.
No kernel may reach another device: no remote copies, remote signals or barrier semaphores. Data moves between devices by JAX's collectives and lax.ppermute only.
A program may use at most 64 MiB of HBM per device.

v0:
```python
import jax
import jax.numpy as jnp
from jax import lax
from jax.sharding import PartitionSpec as P

PANEL = 256
NMAT = 8


def with_halo(value, sides, width):
    for axis, dim in sides:
        devices, length = (lax.axis_size(axis), value.shape[dim])
        up = [(i, (i + 1) % devices) for i in range(devices - 1)]
        down = [(j, i) for i, j in up]
        last = lax.slice_in_dim(value, length - width, length, axis=dim)
        first = lax.slice_in_dim(value, 0, width, axis=dim)
        before = lax.ppermute(last, axis, up)
        after = lax.ppermute(first, axis, down)
        value = jnp.concatenate([before, value, after], axis=dim)
    return value


def couplings(material, blocks):
    kinds = jnp.arange(NMAT, dtype=jnp.int32)
    onehot = (material[..., None] == kinds).astype(jnp.float32)
    table = blocks.reshape(NMAT, 63)
    flat = jnp.einsum("xyzm,mk->xyzk", onehot, table, precision=lax.Precision.HIGHEST)
    return flat.reshape(material.shape + (7, 3, 3))


def neighbours(padded):
    centre = padded[1:-1, 1:-1, 1:-1]
    return [
        centre,
        padded[2:, 1:-1, 1:-1],
        padded[:-2, 1:-1, 1:-1],
        padded[1:-1, 2:, 1:-1],
        padded[1:-1, :-2, 1:-1],
        padded[1:-1, 1:-1, 2:],
        padded[1:-1, 1:-1, :-2],
    ]


def apply_blocks(padded, coupling):
    pieces = neighbours(padded)
    result = jnp.zeros(pieces[0].shape, jnp.float32)
    for offset in range(7):
        result = result + jnp.einsum(
            "xyzij,xyzjc->xyzic",
            coupling[:, :, :, offset],
            pieces[offset],
            precision=lax.Precision.HIGHEST,
        )
    return result


def shards(modes, blocks, material):
    panel = modes[..., :PANEL]
    padded = with_halo(panel, (("row", 0), ("col", 1), ("gz", 2)), 1)
    coupling = couplings(material, blocks)
    stiff_panel = apply_blocks(padded.astype(jnp.float32), coupling).astype(jnp.bfloat16)
    flat_modes = modes.reshape(-1, modes.shape[-1])
    flat_stiff = stiff_panel.reshape(-1, PANEL)
    tile_rows = lax.psum_scatter(
        lax.dot_general(
            flat_modes, flat_stiff, (((0,), (0,)), ((), ())), preferred_element_type=jnp.float32
        ),
        "col",
        scatter_dimension=0,
        tiled=True,
    )
    shared = lax.psum_scatter(tile_rows, "row", scatter_dimension=0, tiled=True)
    summed = lax.psum(shared, "gz")
    reduced = lax.all_gather(summed, "row", axis=0, tiled=True)
    return reduced


def solution(mesh):
    return jax.shard_map(
        shards,
        mesh=mesh,
        in_specs=(P("row", "col", "gz", None, None), P(), P("row", "col", "gz")),
        out_specs=P("col", None),
        check_vma=False,
    )
```

profile of v0, /device:TPU:1, one launch (start us, length us, event | category | flops | bytes accessed | tf_op | source)
XLA Modules:
  0.0 332.2 jit_solution(4879748920144390912)
XLA Ops:
  8.3 4.9 %collective-permute-start.1 = (bf16[1,6,16,3,256]{4,3,2,1,0:T(4,128)(2,1)}, bf16[1,6,16,3,256]{4,3,2,1,0:T(4,128)(2,1)S(1)}, u32[]{:S(2)}, u32[]{:S(2)}) collective-permute-start(bf16[1,6,16,3,256]{4,3,2,1,0:T(4,128)(2,1)} %copy.59), channel_id=1, source_target_pairs={{0,32},{32,64},{64,96},{96,128},{128,160},{160,192},{192,224},{224... | collective-permute-start | bytes 442376 | tf_op jit(solution)/shard_map/ppermute | solution.py:17
  14.0 5.1 %collective-permute-start = (bf16[1,6,16,3,256]{4,3,2,1,0:T(4,128)(2,1)}, bf16[1,6,16,3,256]{4,3,2,1,0:T(4,128)(2,1)S(1)}, u32[]{:S(2)}, u32[]{:S(2)}) collective-permute-start(bf16[1,6,16,3,256]{4,3,2,1,0:T(4,128)(2,1)} %copy.58), channel_id=1, source_target_pairs={{32,0},{64,32},{96,64},{128,96},{160,128},{192,160},{224,192},{256... | collective-permute-start | bytes 442376 | tf_op jit(solution)/shard_map/ppermute | solution.py:18
  22.9 1.6 fusion.18
  24.4 1.4 copy.54
  25.8 2.3 copy.53
  28.1 2.3 copy.52
  30.4 2.3 copy.51
  32.7 2.3 copy.50
  34.9 1.4 copy.49
  40.0 1.6 fusion.10
  41.6 1.6 fusion.8
  43.2 3.9 %collective-permute-done.2 = bf16[6,1,16,3,256]{4,3,2,1,0:T(4,128)(2,1)S(1)} collective-permute-done((bf16[6,1,16,3,256]{4,3,2,1,0:T(4,128)(2,1)S(1)}, bf16[6,1,16,3,256]{4,3,2,1,0:T(4,128)(2,1)S(1)}, u32[]{:S(2)}, u32[]{:S(2)}) %collective-permute-start.2) | collective-permute-done | bytes 147488 | tf_op jit(solution)/shard_map/ppermute | solution.py:18
  47.4 1.4 collective-permute-start.4
  48.8 12.9 %collective-permute-start.5 = (bf16[6,8,1,3,256]{4,1,3,2,0:T(8,128)(2,1)S(1)}, bf16[6,8,1,3,256]{4,1,3,2,0:T(8,128)(2,1)S(1)}, u32[]{:S(2)}, u32[]{:S(2)}) collective-permute-start(bf16[6,8,1,3,256]{4,1,3,2,0:T(8,128)(2,1)S(1)} %copy.38), channel_id=1, source_target_pairs={{0,1},{2,3},{4,5},{6,7},{8,9},{10,11},{12,13},{14,15},{16,17},{18,... | collective-permute-start | bytes 221192 | tf_op jit(solution)/shard_map/ppermute | solution.py:17
  61.7 1.6 fusion.6
  63.3 1.6 fusion.4
  66.1 1.6 fusion.2
  67.7 3.3 add_convert_fusion
  71.0 2.9 convolution_bitcast_fusion
  74.0 93.6 %reduce-scatter.5.cloned.1.call-done = f32[128,256]{0,1:T(8,128)} async-done(((f32[2048,256]{0,1:T(8,128)}), f32[128,256]{0,1:T(8,128)}) %reduce-scatter.5.cloned.1.call-update) | async-done | bytes 131088 | tf_op jit(solution)/shard_map/reduce_scatter | solution.py:64
  167.6 1.7 copy.55
  169.3 99.0 %reduce-scatter.7.cloned.1.call-done = f32[8,256]{1,0:T(8,128)} async-done(((f32[128,256]{1,0:T(8,128)}), f32[8,256]{1,0:T(8,128)}) %reduce-scatter.7.cloned.1.call-update) | async-done | bytes 8208
  269.1 24.8 %psum.7 = f32[8,256]{0,1:T(8,128)S(1)} all-reduce(f32[8,256]{0,1:T(8,128)S(1)} %copy.56), channel_id=1, replica_groups=mesh['row'=16,'col'=16,'gz'=2] {'gz'}, use_global_device_ids=true, to_apply=%region_2.0 | all-reduce | flops 2048 | bytes 16384 | tf_op jit(solution)/shard_map/psum | solution.py:73
  294.0 30.7 %all_gather.3 = f32[128,256]{1,0:T(8,128)S(1)} all-gather(f32[8,256]{1,0:T(8,128)S(1)} %copy.42), channel_id=1, replica_groups=mesh['row'=16,'col'=16,'gz'=2] {'row'}, dimensions={0}, use_global_device_ids=true | all-gather | bytes 139264 | tf_op jit(solution)/shard_map/all_gather | solution.py:74
  (53 shorter events, 12.7 us)
Async XLA Ops:
  6.5 13.8 %copy-start.6 = (s32[4,6,16]{2,0,1:T(4,128)S(1)}, s32[4,6,16]{2,0,1:T(4,128)}, u32[]{:S(2)}) copy-start(s32[4,6,16]{2,0,1:T(4,128)} %param.5) | copy-start | bytes 4612
  6.5 13.8 %copy-start.5 = (f32[8,7,3,3]{1,0,3,2:T(8,128)S(1)}, f32[8,7,3,3]{1,0,3,2:T(8,128)}, u32[]{:S(2)}) copy-start(f32[8,7,3,3]{1,0,3,2:T(8,128)} %param.4) | copy-start | bytes 6052
  6.5 161.1 %reduce-scatter.5.cloned.1.call-start = ((), (), s32[]{:S(2)}) async-start(), calls=%async_computation.2 | async-start | bytes 2228224 | tf_op jit(solution)/shard_map/reduce_scatter | solution.py:64
  8.3 28.0 %collective-permute-start.1 = (bf16[1,6,16,3,256]{4,3,2,1,0:T(4,128)(2,1)}, bf16[1,6,16,3,256]{4,3,2,1,0:T(4,128)(2,1)S(1)}, u32[]{:S(2)}, u32[]{:S(2)}) collective-permute-start(bf16[1,6,16,3,256]{4,3,2,1,0:T(4,128)(2,1)} %copy.59), channel_id=1, source_target_pairs={{0,32},{32,64},{64,96},{96,128},{128,160},{160,192},{192,224},{224... | collective-permute-start | bytes 442376 | tf_op jit(solution)/shard_map/ppermute | solution.py:17
  14.0 23.0 %collective-permute-start = (bf16[1,6,16,3,256]{4,3,2,1,0:T(4,128)(2,1)}, bf16[1,6,16,3,256]{4,3,2,1,0:T(4,128)(2,1)S(1)}, u32[]{:S(2)}, u32[]{:S(2)}) collective-permute-start(bf16[1,6,16,3,256]{4,3,2,1,0:T(4,128)(2,1)} %copy.58), channel_id=1, source_target_pairs={{32,0},{64,32},{96,64},{128,96},{160,128},{192,160},{224,192},{256... | collective-permute-start | bytes 442376 | tf_op jit(solution)/shard_map/ppermute | solution.py:18
  36.4 3.6 %copy-start.3 = (f32[4,6,16,1,3,3]{5,4,2,1,0,3:T(4,128)S(1)}, f32[4,6,16,1,3,3]{5,4,2,1,0,3:T(4,128)}, u32[]{:S(2)}) copy-start(f32[4,6,16,1,3,3]{5,4,2,1,0,3:T(4,128)} %copy.49) | copy-start | bytes 41476
  37.4 5.9 %collective-permute-start.3 = (bf16[6,1,16,3,256]{4,3,2,1,0:T(4,128)(2,1)S(1)}, bf16[6,1,16,3,256]{4,3,2,1,0:T(4,128)(2,1)S(1)}, u32[]{:S(2)}, u32[]{:S(2)}) collective-permute-start(bf16[6,1,16,3,256]{4,3,2,1,0:T(4,128)(2,1)S(1)} %get-tuple-element.9), channel_id=1, source_target_pairs={{0,2},{2,4},{4,6},{6,8},{8,10},{10,12},{12,14},{14,16},{16,18},{18... | collective-permute-start | bytes 442376 | tf_op jit(solution)/shard_map/ppermute | solution.py:17
  38.7 8.5 %collective-permute-start.2 = (bf16[6,1,16,3,256]{4,3,2,1,0:T(4,128)(2,1)S(1)}, bf16[6,1,16,3,256]{4,3,2,1,0:T(4,128)(2,1)S(1)}, u32[]{:S(2)}, u32[]{:S(2)}) collective-permute-start(bf16[6,1,16,3,256]{4,3,2,1,0:T(4,128)(2,1)S(1)} %get-tuple-element.10), channel_id=1, source_target_pairs={{2,0},{4,2},{6,4},{8,6},{10,8},{12,10},{14,12},{16,14},{18,16},{20... | collective-permute-start | bytes 442376 | tf_op jit(solution)/shard_map/ppermute | solution.py:18
  40.0 1.6 copy-start.2
  43.2 18.5 %copy-start.1 = (f32[4,6,16,1,3,3]{5,4,2,1,0,3:T(4,128)S(1)}, f32[4,6,16,1,3,3]{5,4,2,1,0,3:T(4,128)}, u32[]{:S(2)}) copy-start(f32[4,6,16,1,3,3]{5,4,2,1,0,3:T(4,128)} %copy.51) | copy-start | bytes 41476
  47.3 16.0 %copy-start = (f32[4,6,16,1,3,3]{5,4,2,1,0,3:T(4,128)S(1)}, f32[4,6,16,1,3,3]{5,4,2,1,0,3:T(4,128)}, u32[]{:S(2)}) copy-start(f32[4,6,16,1,3,3]{5,4,2,1,0,3:T(4,128)} %copy.52) | copy-start | bytes 41476
  47.4 17.6 %collective-permute-start.4 = (bf16[6,8,1,3,256]{4,1,3,2,0:T(8,128)(2,1)S(1)}, bf16[6,8,1,3,256]{4,1,3,2,0:T(8,128)(2,1)S(1)}, u32[]{:S(2)}, u32[]{:S(2)}) collective-permute-start(bf16[6,8,1,3,256]{4,1,3,2,0:T(8,128)(2,1)S(1)} %copy.34), channel_id=1, source_target_pairs={{1,0},{3,2},{5,4},{7,6},{9,8},{11,10},{13,12},{15,14},{17,16},{19,... | collective-permute-start | bytes 221192 | tf_op jit(solution)/shard_map/ppermute | solution.py:18
  48.8 17.2 %collective-permute-start.5 = (bf16[6,8,1,3,256]{4,1,3,2,0:T(8,128)(2,1)S(1)}, bf16[6,8,1,3,256]{4,1,3,2,0:T(8,128)(2,1)S(1)}, u32[]{:S(2)}, u32[]{:S(2)}) collective-permute-start(bf16[6,8,1,3,256]{4,1,3,2,0:T(8,128)(2,1)S(1)} %copy.38), channel_id=1, source_target_pairs={{0,1},{2,3},{4,5},{6,7},{8,9},{10,11},{12,13},{14,15},{16,17},{18,... | collective-permute-start | bytes 221192 | tf_op jit(solution)/shard_map/ppermute | solution.py:17
  63.3 2.7 copy-start.4
  66.1 5.0 %slice-start = ((s8[4718592]{0:T(1024)(128)(4,1)}), s8[4194304]{0:T(1024)(128)(4,1)S(1)}, s32[]{:S(2)}) async-start(s8[4718592]{0:T(1024)(128)(4,1)} %bitcast.45), calls=%async_computation.4 | async-start | bytes 8388608
  67.7 3.3 %slice-start.1 = ((s8[4718592]{0:T(1024)(128)(4,1)}), s8[524288]{0:T(1024)(128)(4,1)S(1)}, s32[]{:S(2)}) async-start(s8[4718592]{0:T(1024)(128)(4,1)} %bitcast.45), calls=%async_computation.5 | async-start | bytes 1048576
  74.0 194.4 %reduce-scatter.7.cloned.1.call-start = ((), (), s32[]{:S(2)}) async-start(), calls=%async_computation.3 | async-start | bytes 139264
Sparse Core Ops, SparseCore 0:
  74.1 93.4 reduce-scatter.4
  170.6 97.6 reduce-scatter.6
where the time goes:
time: 333 us; the launch traced here: 332 us
  waiting for transfers between devices  198 us (59%)
  blocking collectives  55.5 us (17%)
  starting transfers between devices  27 us (8%)
  local copies, waits for them, and re-layouts  21.9 us (7%)
  matrix products  16.3 us (5%)
  between operations  13.8 us (4%)
    unnamed x3, waiting for transfers between devices  99.1 us
    reduce_scatter x1, waiting for transfers between devices, shards(): lax.psum_scatter(lax.dot_general(flat_modes, flat_stiff, (((0,), (0,)), (...  93.6 us
    all_gather x1, blocking collectives, shards(): reduced = lax.all_gather(summed, 'row', axis=0, tiled=True)  30.7 us
    psum x1, blocking collectives, shards(): summed = lax.psum(shared, 'gz')  24.8 us
    ppermute x3, starting transfers between devices, with_halo(): before = lax.ppermute(last, axis, up)  19.1 us
    dot_general x7, matrix products, apply_blocks(): jnp.einsum('xyzij,xyzjc->xyzic', coupling[:, :, :, offset], pieces[offset...  12.9 us
    squeeze x7, local copies, waits for them, and re-layouts, apply_blocks(): coupling[:, :, :, offset]  12.4 us
    ppermute x3, starting transfers between devices, with_halo(): after = lax.ppermute(first, axis, down)  7.86 us
  transfers between devices with their start and end apart: 8, of which 4 were waited for; matrix products, arithmetic and copies ran while one was open for 8% of the time, Pallas kernels for 0%

commit v1 on v0

--- a/solution.py
+++ b/solution.py
@@ -70,7 +70,8 @@
         tiled=True,
     )
     shared = lax.psum_scatter(tile_rows, "row", scatter_dimension=0, tiled=True)
-    summed = lax.psum(shared, "gz")
+    terms = lax.all_gather(shared, "gz", axis=0, tiled=False)
+    summed = terms.sum(axis=0)
     reduced = lax.all_gather(summed, "row", axis=0, tiled=True)
     return reduced
 

time: 333 us -> 321 us (0.964)
  blocking collectives: 55.5 us -> 46.7 us
    reduce_scatter x0 -> x1, waiting for transfers between devices: none -> 99.1 us  [shards(): shared = lax.psum_scatter(tile_rows, 'row', scatter_dimension=0, tiled=True)]
    unnamed x3 -> x2, waiting for transfers between devices: 99.1 us -> 0.03 us
    psum x1 -> x0, blocking collectives: 24.8 us -> none  [shards(): summed = lax.psum(shared, 'gz')]
    all_gather x0 -> x1, blocking collectives: none -> 12.1 us  [shards(): terms = lax.all_gather(shared, 'gz', axis=0, tiled=False)]
    all_gather x1, blocking collectives: 30.7 us -> 34.6 us  [shards(): reduced = lax.all_gather(summed, 'row', axis=0, tiled=True)]
  transfers between devices with their start and end apart: 8 -> 8, of which waited for: 4 -> 4; matrix products, arithmetic and copies ran while one was open for 8% -> 7% of each run, Pallas kernels for 0% -> 0%
where the time goes in v1:
time: 321 us
  waiting for transfers between devices  197 us (61%)
  blocking collectives  46.7 us (15%)
  starting transfers between devices  27 us (8%)
  local copies, waits for them, and re-layouts  19.3 us (6%)
  matrix products  17.2 us (5%)
  between operations  13.8 us (4%)
    reduce_scatter x1, waiting for transfers between devices, shards(): shared = lax.psum_scatter(tile_rows, 'row', scatter_dimension=0, tiled=True)  99.1 us
    reduce_scatter x1, waiting for transfers between devices, shards(): lax.psum_scatter(lax.dot_general(flat_modes, flat_stiff, (((0,), (0,)), (...  93.6 us
    all_gather x1, blocking collectives, shards(): reduced = lax.all_gather(summed, 'row', axis=0, tiled=True)  34.6 us
    ppermute x3, starting transfers between devices, with_halo(): before = lax.ppermute(last, axis, up)  19.1 us
    dot_general x7, matrix products, apply_blocks(): jnp.einsum('xyzij,xyzjc->xyzic', coupling[:, :, :, offset], pieces[offset...  13.9 us
    all_gather x1, blocking collectives, shards(): terms = lax.all_gather(shared, 'gz', axis=0, tiled=False)  12.1 us
    squeeze x7, local copies, waits for them, and re-layouts, apply_blocks(): coupling[:, :, :, offset]  9.76 us
    ppermute x3, starting transfers between devices, with_halo(): after = lax.ppermute(first, axis, down)  7.86 us
  transfers between devices with their start and end apart: 8, of which 4 were waited for; matrix products, arithmetic and copies ran while one was open for 7% of the time, Pallas kernels for 0%

profile of v1, /device:TPU:1, one launch (start us, length us, event | category | flops | bytes accessed | tf_op | source)
XLA Modules:
  0.0 320.9 jit_solution(611665845469267598)
XLA Ops:
  8.3 4.9 %collective-permute-start.1 = (bf16[1,6,16,3,256]{4,3,2,1,0:T(4,128)(2,1)}, bf16[1,6,16,3,256]{4,3,2,1,0:T(4,128)(2,1)S(1)}, u32[]{:S(2)}, u32[]{:S(2)}) collective-permute-start(bf16[1,6,16,3,256]{4,3,2,1,0:T(4,128)(2,1)} %copy.58), channel_id=1, source_target_pairs={{0,32},{32,64},{64,96},{96,128},{128,160},{160,192},{192,224},{224... | collective-permute-start | bytes 442376 | tf_op jit(solution)/shard_map/ppermute | solution.py:17
  14.1 5.1 %collective-permute-start = (bf16[1,6,16,3,256]{4,3,2,1,0:T(4,128)(2,1)}, bf16[1,6,16,3,256]{4,3,2,1,0:T(4,128)(2,1)}, u32[]{:S(2)}, u32[]{:S(2)}) collective-permute-start(bf16[1,6,16,3,256]{4,3,2,1,0:T(4,128)(2,1)} %copy.57), channel_id=1, source_target_pairs={{32,0},{64,32},{96,64},{128,96},{160,128},{192,160},{224,192},{256... | collective-permute-start | bytes 442376 | tf_op jit(solution)/shard_map/ppermute | solution.py:18
  22.9 1.6 fusion.18
  24.5 2.3 copy.53
  26.8 1.4 copy.52
  28.2 1.4 copy.51
  29.6 1.4 copy.50
  31.0 1.4 copy.49
  32.3 1.4 copy.48
  38.3 2.6 fusion.10
  40.9 1.6 fusion.8
  42.5 2.9 collective-permute-done.2
  45.6 1.4 collective-permute-start.4
  47.1 12.9 %collective-permute-start.5 = (bf16[6,8,1,3,256]{4,1,3,2,0:T(8,128)(2,1)S(1)}, bf16[6,8,1,3,256]{4,1,3,2,0:T(8,128)(2,1)S(1)}, u32[]{:S(2)}, u32[]{:S(2)}) collective-permute-start(bf16[6,8,1,3,256]{4,1,3,2,0:T(8,128)(2,1)S(1)} %copy.37), channel_id=1, source_target_pairs={{0,1},{2,3},{4,5},{6,7},{8,9},{10,11},{12,13},{14,15},{16,17},{18,... | collective-permute-start | bytes 221192 | tf_op jit(solution)/shard_map/ppermute | solution.py:17
  60.0 1.6 fusion.6
  61.6 1.6 fusion.4
  64.4 1.6 fusion.2
  66.0 3.3 %add_convert_fusion = bf16[4,6,16,3,256]{4,3,2,1,0:T(4,128)(2,1)S(1)} fusion(f32[4,6,16,3,256]{4,3,2,1,0:T(4,128)S(1)} %fusion.2, f32[4,6,16,3,256]{4,3,2,1,0:T(4,128)S(1)} %fusion.4, f32[4,6,16,3,256]{4,3,2,1,0:T(4,128)S(1)} %fusion.6, f32[4,6,16,3,256]{4,3,2,1,0:T(4,128)S(1)} %fusion.8, f32[4,6,16,3,256]{4,3,2,1,0:T(4,128)S(1)} %fusion.18, ...), kind=kOutput, calls=%fused_computation.1 | convolution fusion | flops 15040512 | bytes 8934912 | tf_op jit(solution)/shard_map/xyzij,xyzjc->xyzic/dot_general | solution.py:48
  69.4 2.9 convolution_bitcast_fusion
  72.3 93.6 %reduce-scatter.5.cloned.1.call-done = f32[128,256]{0,1:T(8,128)} async-done(((f32[2048,256]{0,1:T(8,128)}), f32[128,256]{0,1:T(8,128)}) %reduce-scatter.5.cloned.1.call-update) | async-done | bytes 131088 | tf_op jit(solution)/shard_map/reduce_scatter | solution.py:64
  165.9 1.7 copy.54
  167.6 99.1 %reduce-scatter.7.cloned.1.call-done = f32[8,256]{1,0:T(8,128)} async-done(((f32[128,256]{1,0:T(8,128)}), f32[8,256]{1,0:T(8,128)}) %reduce-scatter.7.cloned.1.call-update) | async-done | bytes 8208 | tf_op jit(solution)/shard_map/reduce_scatter | solution.py:72
  266.6 12.1 %all-gather = f32[16,256]{1,0:T(8,128)S(1)} all-gather(f32[8,256]{1,0:T(8,128)} %reduce-scatter.7.cloned.1.call-done), channel_id=2, replica_groups=mesh['row'=16,'col'=16,'gz'=2] {'gz'}, dimensions={0}, use_global_device_ids=true | all-gather | bytes 24576 | tf_op jit(solution)/shard_map/all_gather | solution.py:73
  278.8 34.6 %all_gather.11 = f32[128,256]{1,0:T(8,128)S(1)} all-gather(f32[8,256]{1,0:T(8,128)S(1)} %bitcast_reduce_fusion), channel_id=1, replica_groups=mesh['row'=16,'col'=16,'gz'=2] {'row'}, dimensions={0}, use_global_device_ids=true | all-gather | bytes 139264 | tf_op jit(solution)/shard_map/all_gather | solution.py:75
  (60 shorter events, 12.7 us)
Async XLA Ops:
  6.5 13.8 %copy-start.10 = (s32[4,6,16]{2,0,1:T(4,128)S(1)}, s32[4,6,16]{2,0,1:T(4,128)}, u32[]{:S(2)}) copy-start(s32[4,6,16]{2,0,1:T(4,128)} %param.5) | copy-start | bytes 4612
  6.5 13.8 %copy-start.9 = (f32[8,7,3,3]{1,0,3,2:T(8,128)S(1)}, f32[8,7,3,3]{1,0,3,2:T(8,128)}, u32[]{:S(2)}) copy-start(f32[8,7,3,3]{1,0,3,2:T(8,128)} %param.4) | copy-start | bytes 6052
  6.5 159.4 %reduce-scatter.5.cloned.1.call-start = ((), (), s32[]{:S(2)}) async-start(), calls=%async_computation.2 | async-start | bytes 2228224 | tf_op jit(solution)/shard_map/reduce_scatter | solution.py:64
  8.3 25.4 %collective-permute-start.1 = (bf16[1,6,16,3,256]{4,3,2,1,0:T(4,128)(2,1)}, bf16[1,6,16,3,256]{4,3,2,1,0:T(4,128)(2,1)S(1)}, u32[]{:S(2)}, u32[]{:S(2)}) collective-permute-start(bf16[1,6,16,3,256]{4,3,2,1,0:T(4,128)(2,1)} %copy.58), channel_id=1, source_target_pairs={{0,32},{32,64},{64,96},{96,128},{128,160},{160,192},{192,224},{224... | collective-permute-start | bytes 442376 | tf_op jit(solution)/shard_map/ppermute | solution.py:17
  14.1 20.4 %collective-permute-start = (bf16[1,6,16,3,256]{4,3,2,1,0:T(4,128)(2,1)}, bf16[1,6,16,3,256]{4,3,2,1,0:T(4,128)(2,1)}, u32[]{:S(2)}, u32[]{:S(2)}) collective-permute-start(bf16[1,6,16,3,256]{4,3,2,1,0:T(4,128)(2,1)} %copy.57), channel_id=1, source_target_pairs={{32,0},{64,32},{96,64},{128,96},{160,128},{192,160},{224,192},{256... | collective-permute-start | bytes 442376 | tf_op jit(solution)/shard_map/ppermute | solution.py:18
  22.9 3.9 %copy-start.8 = (f32[4,6,16,1,3,3]{2,3,5,4,1,0:T(1,128)S(1)}, f32[4,6,16,1,3,3]{2,3,5,4,1,0:T(1,128)}, u32[]{:S(2)}) copy-start(f32[4,6,16,1,3,3]{2,3,5,4,1,0:T(1,128)} %get-tuple-element.12) | copy-start | bytes 41476
  24.4 3.8 %copy-start.7 = (f32[4,6,16,1,3,3]{2,3,5,4,1,0:T(1,128)S(1)}, f32[4,6,16,1,3,3]{2,3,5,4,1,0:T(1,128)}, u32[]{:S(2)}) copy-start(f32[4,6,16,1,3,3]{2,3,5,4,1,0:T(1,128)} %get-tuple-element.13) | copy-start | bytes 41476
  24.5 5.1 %copy-start.6 = (f32[4,6,16,1,3,3]{2,3,5,4,1,0:T(1,128)S(1)}, f32[4,6,16,1,3,3]{2,3,5,4,1,0:T(1,128)}, u32[]{:S(2)}) copy-start(f32[4,6,16,1,3,3]{2,3,5,4,1,0:T(1,128)} %get-tuple-element.14) | copy-start | bytes 41476
  33.8 4.5 %copy-start.4 = (f32[4,6,16,1,3,3]{5,4,2,1,0,3:T(4,128)S(1)}, f32[4,6,16,1,3,3]{5,4,2,1,0,3:T(4,128)}, u32[]{:S(2)}) copy-start(f32[4,6,16,1,3,3]{5,4,2,1,0,3:T(4,128)} %copy.48) | copy-start | bytes 41476
  35.7 6.9 %collective-permute-start.3 = (bf16[6,1,16,3,256]{4,3,2,1,0:T(4,128)(2,1)S(1)}, bf16[6,1,16,3,256]{4,3,2,1,0:T(4,128)(2,1)S(1)}, u32[]{:S(2)}, u32[]{:S(2)}) collective-permute-start(bf16[6,1,16,3,256]{4,3,2,1,0:T(4,128)(2,1)S(1)} %get-tuple-element.9), channel_id=1, source_target_pairs={{0,2},{2,4},{4,6},{6,8},{8,10},{10,12},{12,14},{14,16},{16,18},{18... | collective-permute-start | bytes 442376 | tf_op jit(solution)/shard_map/ppermute | solution.py:17
  37.0 8.5 %collective-permute-start.2 = (bf16[6,1,16,3,256]{4,3,2,1,0:T(4,128)(2,1)S(1)}, bf16[6,1,16,3,256]{4,3,2,1,0:T(4,128)(2,1)S(1)}, u32[]{:S(2)}, u32[]{:S(2)}) collective-permute-start(bf16[6,1,16,3,256]{4,3,2,1,0:T(4,128)(2,1)S(1)} %get-tuple-element.10), channel_id=1, source_target_pairs={{2,0},{4,2},{6,4},{8,6},{10,8},{12,10},{14,12},{16,14},{18,16},{20... | collective-permute-start | bytes 442376 | tf_op jit(solution)/shard_map/ppermute | solution.py:18
  38.3 2.6 copy-start.3
  42.5 17.5 %copy-start.2 = (f32[4,6,16,1,3,3]{5,4,2,1,0,3:T(4,128)S(1)}, f32[4,6,16,1,3,3]{5,4,2,1,0,3:T(4,128)}, u32[]{:S(2)}) copy-start(f32[4,6,16,1,3,3]{5,4,2,1,0,3:T(4,128)} %copy.50) | copy-start | bytes 41476
  45.6 16.0 %copy-start.1 = (f32[4,6,16,1,3,3]{5,4,2,1,0,3:T(4,128)S(1)}, f32[4,6,16,1,3,3]{5,4,2,1,0,3:T(4,128)}, u32[]{:S(2)}) copy-start(f32[4,6,16,1,3,3]{5,4,2,1,0,3:T(4,128)} %copy.51) | copy-start | bytes 41476
  45.6 17.6 %collective-permute-start.4 = (bf16[6,8,1,3,256]{4,1,3,2,0:T(8,128)(2,1)S(1)}, bf16[6,8,1,3,256]{4,1,3,2,0:T(8,128)(2,1)S(1)}, u32[]{:S(2)}, u32[]{:S(2)}) collective-permute-start(bf16[6,8,1,3,256]{4,1,3,2,0:T(8,128)(2,1)S(1)} %copy.33), channel_id=1, source_target_pairs={{1,0},{3,2},{5,4},{7,6},{9,8},{11,10},{13,12},{15,14},{17,16},{19,... | collective-permute-start | bytes 221192 | tf_op jit(solution)/shard_map/ppermute | solution.py:18
  47.1 17.2 %collective-permute-start.5 = (bf16[6,8,1,3,256]{4,1,3,2,0:T(8,128)(2,1)S(1)}, bf16[6,8,1,3,256]{4,1,3,2,0:T(8,128)(2,1)S(1)}, u32[]{:S(2)}, u32[]{:S(2)}) collective-permute-start(bf16[6,8,1,3,256]{4,1,3,2,0:T(8,128)(2,1)S(1)} %copy.37), channel_id=1, source_target_pairs={{0,1},{2,3},{4,5},{6,7},{8,9},{10,11},{12,13},{14,15},{16,17},{18,... | collective-permute-start | bytes 221192 | tf_op jit(solution)/shard_map/ppermute | solution.py:17
  61.6 2.7 copy-start.5
  64.3 1.6 copy-start
  64.4 5.0 %slice-start = ((s8[4718592]{0:T(1024)(128)(4,1)}), s8[4194304]{0:T(1024)(128)(4,1)S(1)}, s32[]{:S(2)}) async-start(s8[4718592]{0:T(1024)(128)(4,1)} %bitcast.47), calls=%async_computation.4 | async-start | bytes 8388608
  66.0 3.3 %slice-start.1 = ((s8[4718592]{0:T(1024)(128)(4,1)}), s8[524288]{0:T(1024)(128)(4,1)S(1)}, s32[]{:S(2)}) async-start(s8[4718592]{0:T(1024)(128)(4,1)} %bitcast.47), calls=%async_computation.5 | async-start | bytes 1048576
  72.2 194.4 %reduce-scatter.7.cloned.1.call-start = ((), (), s32[]{:S(2)}) async-start(), calls=%async_computation.3 | async-start | bytes 139264 | tf_op jit(solution)/shard_map/reduce_scatter | solution.py:72
Sparse Core Ops, SparseCore 0:
  72.4 93.4 reduce-scatter.4
  168.9 97.6 reduce-scatter.6
